TPU v7x, 32 devices: a whole 2x2x4 slice. The times are simulated.
32 devices in a mesh: hour: 16 (over z, y, x), region: 2 (over core).
Axes of the slice: x: 2, y: 2, z: 4, core: 2. Of those that a mesh axis runs over, the one named last changes fastest.
Arguments:
- demand: float32 [2240, 1024], P('hour', 'region'), may hold values from 0.2 to 2
- avail_factor: bfloat16 [2240, 8, 1024], P('hour', None, 'region'), may hold values from 0 to 1
- tech_mask: int32 [8, 1024], P(None, 'region'), may hold values 0 or 1
- var_cost: float32 [8, 1024], P(None, 'region'), may hold values from 0.1 to 2
- inv_cost: float32 [8, 1024], P(None, 'region'), may hold values from 0.2 to 1
- ramp_rate: float32 [8, 1024], P(None, 'region'), may hold values from 0.1 to 1
- network: float32 [1024, 1024], P('region'), as said below
- pattern: int32 [8, 8], replicated, may hold values from 0 to 1, as said below
- live_hours: int32 [1], replicated, may hold values from 1961 to 2100
- generation: float32 [2240, 8, 1024], P('hour', None, 'region'), may hold values from 0 to 1
- angles: float32 [2240, 1024], P('hour', 'region'), may hold values from -3 to 3
- levels: float32 [2240, 1024], P('hour', 'region'), may hold values from 0 to 2
- net_power: float32 [2240, 1024], P('hour', 'region'), may hold values from -3 to 3
- capacity: float32 [8, 1024], P(None, 'region'), may hold values from 0.5 to 2
- balance_dual: float32 [2240, 1024], P('hour', 'region'), may hold values from -3 to 3
- storage_dual: float32 [2240, 1024], P('hour', 'region'), may hold values from -3 to 3
- limit_dual: float32 [2240, 8, 1024], P('hour', None, 'region'), may hold values from 0 to 1.5
- ramp_dual: float32 [2240, 8, 1024], P('hour', None, 'region'), may hold values from 0 to 0.5
Outputs:
- final_generation: float32 [2240, 8, 1024], P('hour', None, 'region')
- final_angles: float32 [2240, 1024], P('hour', 'region')
- final_levels: float32 [2240, 1024], P('hour', 'region')
- final_power: float32 [2240, 1024], P('hour', 'region')
- final_capacity: float32 [8, 1024], P(None, 'region')
- final_balance: float32 [2240, 1024], P('hour', 'region')
- final_storage: float32 [2240, 1024], P('hour', 'region')
- final_limit: float32 [2240, 8, 1024], P('hour', None, 'region')
- final_ramp: float32 [2240, 8, 1024], P('hour', None, 'region')
Inputs may be any that keep to these rules, and one draw needn't show every extreme that they name: pattern is symmetric with ones on its diagonal. network is symmetric.
All inputs are finite; a program needn't handle non-finite values. No bound on the sum of `tech_mask` on one device may be relied on, other than what follows from the above.
Results may differ from a plain program's by a relative error of at most 0.0003.
Values sent between devices are 32-bit elements; how exact they have to be, the bound alone decides.
No kernel may reach another device: no remote copies, remote signals or barrier semaphores. Data moves between devices by JAX's collectives and lax.ppermute only.
A program may use at most 64 MiB of HBM per device.

v0:
```python
import jax
import jax.numpy as jnp
from jax import lax
from jax.sharding import PartitionSpec as P

BUS = 1024
TECH = 8
BLOCK = 128
ITERS = 2
primal_step = 0.2
capacity_step = 4.0
dual_scale = 0.06


def shifted(block, axis, distance):
    devices = range(lax.axis_size(axis))
    route = [((i - distance) % len(devices), i) for i in devices]
    return lax.ppermute(block, axis, route)


def per_device(
    demand,
    avail_factor,
    tech_mask,
    var_cost,
    inv_cost,
    ramp_rate,
    network,
    pattern,
    live_hours,
    generation,
    angles,
    levels,
    net_power,
    capacity,
    balance_dual,
    storage_dual,
    limit_dual,
    ramp_dual,
):
    hour_rows = demand.shape[0]
    local_bus = demand.shape[1]
    total_hours = hour_rows * lax.axis_size("hour")
    first_hour = lax.axis_index("hour") * hour_rows
    live_rows = (first_hour + jnp.arange(hour_rows, dtype=jnp.int32) < live_hours[0]).astype(
        jnp.float32
    )
    available = (
        avail_factor.astype(jnp.float32)
        * tech_mask.astype(jnp.float32)[None]
        * live_rows[:, None, None]
    )
    live_load = demand * live_rows[:, None]
    blocks_here = local_bus // BLOCK
    pattern_rows = lax.dynamic_slice_in_dim(
        pattern, lax.axis_index("region") * blocks_here, blocks_here, 0
    )
    block_mask = jnp.repeat(jnp.repeat(pattern_rows.astype(jnp.float32), BLOCK, 0), BLOCK, 1)
    matrix = network * block_mask
    entry_count = float(total_hours * (TECH + 3) * BUS)

    def fold_part(segment):
        return lax.dot_general(
            segment,
            matrix,
            (((1,), (1,)), ((), ())),
            precision=lax.Precision.HIGHEST,
            preferred_element_type=jnp.float32,
        )

    for iteration in range(ITERS):
        behind = shifted((ramp_dual[-1:], storage_dual[-1:]), "hour", 1)
        prev_ramp = jnp.concatenate([behind[0], ramp_dual[:-1]], axis=0)
        prev_store = jnp.concatenate([behind[1], storage_dual[:-1]], axis=0)
        gen_new = jnp.maximum(
            0.0,
            generation
            - primal_step
            * (var_cost[None] + balance_dual[:, None, :] + limit_dual + prev_ramp - ramp_dual),
        )
        ang_new = angles + primal_step * fold_part(
            lax.all_gather(balance_dual, "region", axis=1, tiled=True)
        )
        pow_new = net_power - primal_step * (balance_dual + storage_dual)
        lev_new = jnp.maximum(0.0, levels - primal_step * (prev_store - storage_dual))
        square_part = (
            jnp.sum((gen_new - generation) ** 2)
            + jnp.sum((ang_new - angles) ** 2)
            + jnp.sum((pow_new - net_power) ** 2)
            + jnp.sum((lev_new - levels) ** 2)
        )
        invest_part = jnp.sum(available * limit_dual + ramp_rate[None] * ramp_dual, axis=0)
        invest = lax.psum(invest_part, "hour")
        squares = lax.psum(square_part, ("hour", "region"))
        cap_new = jnp.maximum(
            0.0, capacity - capacity_step * (inv_cost - invest / float(total_hours))
        )
        step_size = jnp.sqrt(squares / entry_count + 1e-06)
        dual_step = dual_scale / step_size
        gen_bar = 2.0 * gen_new - generation
        ang_bar = 2.0 * ang_new - angles
        pow_bar = 2.0 * pow_new - net_power
        lev_bar = 2.0 * lev_new - levels
        cap_bar = 2.0 * cap_new - capacity
        forward = shifted((gen_bar[:1], lev_bar[:1]), "hour", -1)
        next_gen = jnp.concatenate([gen_bar[1:], forward[0]], axis=0)
        next_level = jnp.concatenate([lev_bar[1:], forward[1]], axis=0)
        balance_dual = balance_dual + dual_step * (
            jnp.sum(gen_bar, axis=1)
            + pow_bar
            - fold_part(lax.all_gather(ang_bar, "region", axis=1, tiled=True))
            - live_load
        )
        storage_dual = storage_dual + dual_step * (next_level - lev_bar + pow_bar)
        limit_dual = jnp.maximum(
            0.0, limit_dual + dual_step * (gen_bar - available * cap_bar[None])
        )
        ramp_dual = jnp.maximum(
            0.0, ramp_dual + dual_step * (next_gen - gen_bar - ramp_rate[None] * cap_bar[None])
        )
        generation, angles, net_power, levels, capacity = (
            gen_new,
            ang_new,
            pow_new,
            lev_new,
            cap_new,
        )
    return (
        generation,
        angles,
        levels,
        net_power,
        capacity,
        balance_dual,
        storage_dual,
        limit_dual,
        ramp_dual,
    )


def solution(mesh):
    return jax.shard_map(
        per_device,
        mesh=mesh,
        in_specs=(
            P("hour", "region"),
            P("hour", None, "region"),
            P(None, "region"),
            P(None, "region"),
            P(None, "region"),
            P(None, "region"),
            P("region", None),
            P(),
            P(),
            P("hour", None, "region"),
            P("hour", "region"),
            P("hour", "region"),
            P("hour", "region"),
            P(None, "region"),
            P("hour", "region"),
            P("hour", "region"),
            P("hour", None, "region"),
            P("hour", None, "region"),
        ),
        out_specs=(
            P("hour", None, "region"),
            P("hour", "region"),
            P("hour", "region"),
            P("hour", "region"),
            P(None, "region"),
            P("hour", "region"),
            P("hour", "region"),
            P("hour", None, "region"),
            P("hour", None, "region"),
        ),
        check_vma=False,
    )
```

profile of v0, /device:TPU:0, one launch (start us, length us, event | category | flops | bytes accessed | tf_op | source)
XLA Modules:
  0.0 319.3 jit_solution(14245832103954252068)
XLA Ops:
  1.4 2.9 collective-permute-start.1
  7.2 2.4 all_gather.12
  12.2 3.7 %multiply_subtract_fusion.7 = (f32[140,512]{1,0:T(8,128)S(1)}, f32[]{:T(128)}, f32[140,512]{1,0:T(8,128)}) fusion(f32[140,512]{1,0:T(8,128)S(1)} %copy-done.28, f32[512,1024]{1,0:T(8,128)S(1)} %bitcast_multiply_fusion, f32[140,1024]{1,0:T(8,128)S(1)} %all_gather.12), kind=kOutput, calls=%fused_computation.61 | convolution fusion | flops 881305600 | bytes 3530756 | tf_op jit(solution)/shard_map/dot_general | solution.py:63
  15.9 2.2 all_gather.13
  18.1 3.0 fusion.39
  22.3 3.0 multiply_subtract_fusion.6
  26.1 4.1 %collective-permute-start.4 = (f32[1,512]{1,0:T(1,128)S(1)}, f32[1,512]{1,0:T(1,128)S(1)}, u32[]{:S(2)}, u32[]{:S(2)}) collective-permute-start(f32[1,512]{1,0:T(1,128)S(1)} %slice.69), channel_id=1, source_target_pairs={{2,0},{4,2},{6,4},{8,6},{10,8},{12,10},{14,12},{16,14},{18,16},{20... | collective-permute-start | bytes 6152 | tf_op jit(solution)/shard_map/ppermute | solution.py:18
  30.2 6.1 %fusion.36 = (f32[140,512]{1,0:T(8,128)}, f32[140,8,512]{2,1,0:T(8,128)}, f32[140,8,512]{2,1,0:T(8,128)S(1)}, f32[8,512]{1,0:T(8,128)S(1)}) fusion(f32[140,8,512]{2,1,0:T(8,128)} %param.27, f32[140,8,512]{2,1,0:T(8,128)S(1)} %copy-done.5, f32[139,8,512]{2,1,0:T(8,128)S(1)} %slice-done, f32[1,8,512]{2,1,0:T(8,128)S(1)} %collective-permute-done, ...), kind=kLoop, calls=%fused_computation.74 | loop fusion | flops 10246144 | bytes 15548976 | tf_op jit(solution)/shard_map/reduce_sum | solution.py:109
  41.9 37.6 %psum.28 = f32[]{:T(128)} all-reduce(f32[]{:T(128)S(6)} %add.149), channel_id=1, replica_groups=mesh['hour'=16,'region'=2] {'hour','region'}, use_global_device_ids=true, to_apply=%region_4.0 | all-reduce | flops 1 | bytes 8 | tf_op jit(solution)/shard_map/psum | solution.py:94
  80.3 3.3 %multiply_reduce_fusion.3 = (f32[]{:T(128)}, f32[140,512]{1,0:T(8,128)}, f32[140,512]{1,0:T(8,128)S(1)}, f32[140,512]{1,0:T(8,128)}) fusion(f32[140,512]{1,0:T(8,128)} %get-tuple-element.42, f32[140,512]{1,0:T(8,128)} %param.33, f32[140,512]{1,0:T(8,128)} %param.30, f32[140,512]{1,0:T(8,128)} %copy-done.20, f32[1,512]{1,0:T(1,128)S(1)} %collective-permute-done.4, ...), kind=kLoop, calls=%fused_computation.56 | loop fusion | flops 1361919 | bytes 3441208 | tf_op jit(solution)/shard_map/reduce_sum | solution.py:89
  84.3 2.3 collective-permute-start.5
  86.6 75.0 %psum.29 = f32[8,512]{1,0:T(8,128)S(1)} all-reduce(f32[8,512]{1,0:T(8,128)S(1)} %get-tuple-element.32), channel_id=1, replica_groups=mesh['hour'=16,'region'=2] {'hour'}, use_global_device_ids=true, to_apply=%region_7.0 | all-reduce | flops 4096 | bytes 32768 | tf_op jit(solution)/shard_map/psum | solution.py:93
  162.4 2.6 all_gather.14
  165.0 4.8 %multiply_reduce_fusion.4 = (f32[]{:T(128)}, f32[140,512]{1,0:T(8,128)}, f32[140,512]{1,0:T(8,128)}) fusion(f32[140,512]{1,0:T(8,128)} %get-tuple-element.43, f32[140,1024]{1,0:T(8,128)S(1)} %all_gather.14, f32[512,1024]{1,0:T(8,128)S(1)} %bitcast_multiply_fusion), kind=kOutput, calls=%fused_computation.57 | convolution fusion | flops 881305600 | bytes 3530756 | tf_op jit(solution)/shard_map/dot_general | solution.py:63
  172.6 2.1 collective-permute-start.3
  175.5 4.4 %collective-permute-done.3 = f32[1,8,512]{2,1,0:T(8,128)S(1)} collective-permute-done((f32[1,8,512]{2,1,0:T(8,128)S(1)}, f32[1,8,512]{2,1,0:T(8,128)S(1)}, u32[]{:S(2)}, u32[]{:S(2)}) %collective-permute-start.3) | collective-permute-done | bytes 16416 | tf_op jit(solution)/shard_map/ppermute | solution.py:18
  180.0 4.3 %multiply_reduce_fusion = (f32[]{:T(128)}, f32[140,8,512]{2,1,0:T(8,128)}, f32[140,8,512]{2,1,0:T(8,128)}) fusion(f32[140,8,512]{2,1,0:T(8,128)S(1)} %copy-done.3, f32[140,8,512]{2,1,0:T(8,128)S(1)} %fusion.7, f32[139,8,512]{2,1,0:T(8,128)S(1)} %slice.67, f32[1,8,512]{2,1,0:T(8,128)S(1)} %collective-permute-done.3, f32[140,512]{1,0:T(8,128)S(1)} %copy-done.16, ...), kind=kLoop, calls=%fused_computation.22 | loop fusion | flops 10895359 | bytes 17539640 | tf_op jit(solution)/shard_map/reduce_sum | solution.py:87
  186.8 3.9 %all_gather.15 = f32[140,1024]{1,0:T(8,128)} all-gather(f32[140,512]{1,0:T(8,128)} %get-tuple-element.38), channel_id=1, replica_groups=mesh['hour'=16,'region'=2] {'region'}, dimensions={1}, use_global_device_ids=true | all-gather | bytes 860160 | tf_op jit(solution)/shard_map/all_gather | solution.py:111
  190.7 36.8 %psum.31 = f32[]{:T(128)} all-reduce(f32[]{:T(128)S(6)} %add.169), channel_id=1, replica_groups=mesh['hour'=16,'region'=2] {'hour','region'}, use_global_device_ids=true, to_apply=%region_14.0 | all-reduce | flops 1 | bytes 8 | tf_op jit(solution)/shard_map/psum | solution.py:94
  228.2 2.2 add_reduce_fusion
  230.4 75.8 %psum.30 = f32[8,512]{1,0:T(8,128)S(1)} all-reduce(f32[8,512]{1,0:T(8,128)S(1)} %add_reduce_fusion), channel_id=1, replica_groups=mesh['hour'=16,'region'=2] {'hour'}, use_global_device_ids=true, to_apply=%region_9.0 | all-reduce | flops 4096 | bytes 32768 | tf_op jit(solution)/shard_map/psum | solution.py:93
  306.9 5.3 %add_maximum_fusion = (f32[140,8,512]{2,1,0:T(8,128)}, f32[140,8,512]{2,1,0:T(8,128)S(1)}) fusion(f32[140,8,512]{2,1,0:T(8,128)} %get-tuple-element.22, bf16[140,8,512]{2,1,0:T(8,128)(2,1)S(1)} %copy-done.7, f32[8,512]{1,0:T(8,128)S(1)} %get-tuple-element.10, f32[]{:T(128)S(6)} %div.23, f32[140]{0:T(256)} %copy-done.33, ...), kind=kLoop, calls=%fused_computation.20 | loop fusion | flops 5734400 | bytes 12649012 | tf_op jit(solution)/shard_map/max | solution.py:115
  312.2 2.3 fusion.40
  316.0 2.3 fusion.15
  (114 shorter events, 18.6 us)
Async XLA Ops:
  1.4 20.5 %collective-permute-start.1 = (f32[1,512]{1,0:T(1,128)S(1)}, f32[1,512]{1,0:T(1,128)S(1)}, u32[]{:S(2)}, u32[]{:S(2)}) collective-permute-start(f32[1,512]{1,0:T(1,128)S(1)} %slice.50), channel_id=1, source_target_pairs={{30,0},{0,2},{2,4},{4,6},{6,8},{8,10},{10,12},{12,14},{14,16},{16,... | collective-permute-start | bytes 6152 | tf_op jit(solution)/shard_map/ppermute | solution.py:18
  5.0 25.2 %collective-permute-start = (f32[1,8,512]{2,1,0:T(8,128)S(1)}, f32[1,8,512]{2,1,0:T(8,128)S(1)}, u32[]{:S(2)}, u32[]{:S(2)}) collective-permute-start(f32[1,8,512]{2,1,0:T(8,128)S(1)} %slice.48), channel_id=1, source_target_pairs={{30,0},{0,2},{2,4},{4,6},{6,8},{8,10},{10,12},{12,14},{14,16},{16,... | collective-permute-start | bytes 49160 | tf_op jit(solution)/shard_map/ppermute | solution.py:18
  12.2 152.8 %copy-start = (f32[512,1024]{1,0:T(8,128)}, f32[512,1024]{1,0:T(8,128)S(1)}, u32[]{:S(2)}) copy-start(f32[512,1024]{1,0:T(8,128)S(1)} %bitcast_multiply_fusion) | copy-start | bytes 6291460
  21.1 59.1 %copy-start.33 = (f32[140]{0:T(256)}, f32[140]{0:T(256)S(1)}, u32[]{:S(2)}) copy-start(f32[140]{0:T(256)S(1)} %compare_convert_fusion) | copy-start | bytes 1684
  21.2 9.0 %copy-start.5 = (f32[140,8,512]{2,1,0:T(8,128)S(1)}, f32[140,8,512]{2,1,0:T(8,128)}, u32[]{:S(2)}) copy-start(f32[140,8,512]{2,1,0:T(8,128)} %param.35) | copy-start | bytes 6881284
  21.2 9.0 %copy-start.7 = (bf16[140,8,512]{2,1,0:T(8,128)(2,1)S(1)}, bf16[140,8,512]{2,1,0:T(8,128)(2,1)}, u32[]{:S(2)}) copy-start(bf16[140,8,512]{2,1,0:T(8,128)(2,1)} %param.19) | copy-start | bytes 3440644
  21.9 8.4 %slice-start = ((f32[140,8,512]{2,1,0:T(8,128)}), f32[139,8,512]{2,1,0:T(8,128)S(1)}, s32[]{:S(2)}) async-start(f32[140,8,512]{2,1,0:T(8,128)} %param.35), calls=%async_computation | async-start | bytes 4554752 | tf_op jit(solution)/shard_map/slice | solution.py:73
  21.9 8.4 %copy-start.29 = (f32[8,512]{1,0:T(8,128)S(1)}, f32[8,512]{1,0:T(8,128)}, u32[]{:S(2)}) copy-start(f32[8,512]{1,0:T(8,128)} %param.23) | copy-start | bytes 49156
  21.9 8.4 %copy-start.32 = (f32[8,512]{1,0:T(8,128)S(1)}, f32[8,512]{1,0:T(8,128)}, u32[]{:S(2)}) copy-start(f32[8,512]{1,0:T(8,128)} %param.21) | copy-start | bytes 49156
  25.3 4.8 %copy-start.13 = (f32[140,512]{1,0:T(8,128)}, f32[140,512]{1,0:T(8,128)S(1)}, u32[]{:S(2)}) copy-start(f32[140,512]{1,0:T(8,128)S(1)} %get-tuple-element.24) | copy-start | bytes 860164
  26.1 10.3 %copy-start.8 = (f32[140,8,512]{2,1,0:T(8,128)S(1)}, f32[140,8,512]{2,1,0:T(8,128)}, u32[]{:S(2)}) copy-start(f32[140,8,512]{2,1,0:T(8,128)} %param.27) | copy-start | bytes 6881284
  26.1 54.2 %collective-permute-start.4 = (f32[1,512]{1,0:T(1,128)S(1)}, f32[1,512]{1,0:T(1,128)S(1)}, u32[]{:S(2)}, u32[]{:S(2)}) collective-permute-start(f32[1,512]{1,0:T(1,128)S(1)} %slice.69), channel_id=1, source_target_pairs={{2,0},{4,2},{6,4},{8,6},{10,8},{12,10},{14,12},{16,14},{18,16},{20... | collective-permute-start | bytes 6152 | tf_op jit(solution)/shard_map/ppermute | solution.py:18
  83.6 86.2 %copy-start.30 = (f32[8,512]{1,0:T(8,128)S(1)}, f32[8,512]{1,0:T(8,128)}, u32[]{:S(2)}) copy-start(f32[8,512]{1,0:T(8,128)} %param.31) | copy-start | bytes 49156
  83.6 86.2 %copy-start.31 = (f32[8,512]{1,0:T(8,128)S(1)}, f32[8,512]{1,0:T(8,128)}, u32[]{:S(2)}) copy-start(f32[8,512]{1,0:T(8,128)} %param.22) | copy-start | bytes 49156
  84.3 85.8 %collective-permute-start.5 = (f32[1,512]{1,0:T(1,128)S(1)}, f32[1,512]{1,0:T(1,128)S(1)}, u32[]{:S(2)}, u32[]{:S(2)}) collective-permute-start(f32[1,512]{1,0:T(1,128)S(1)} %slice.70), channel_id=1, source_target_pairs={{30,0},{0,2},{2,4},{4,6},{6,8},{8,10},{10,12},{12,14},{14,16},{16,... | collective-permute-start | bytes 6152 | tf_op jit(solution)/shard_map/ppermute | solution.py:18
  161.5 8.3 %copy-start.4 = (f32[140,8,512]{2,1,0:T(8,128)S(1)}, f32[140,8,512]{2,1,0:T(8,128)}, u32[]{:S(2)}) copy-start(f32[140,8,512]{2,1,0:T(8,128)} %get-tuple-element.26) | copy-start | bytes 6881284
  162.4 9.3 %collective-permute-start.2 = (f32[1,8,512]{2,1,0:T(8,128)S(1)}, f32[1,8,512]{2,1,0:T(8,128)S(1)}, u32[]{:S(2)}, u32[]{:S(2)}) collective-permute-start(f32[1,8,512]{2,1,0:T(8,128)S(1)} %slice.65), channel_id=1, source_target_pairs={{2,0},{4,2},{6,4},{8,6},{10,8},{12,10},{14,12},{16,14},{18,16},{20... | collective-permute-start | bytes 49160 | tf_op jit(solution)/shard_map/ppermute | solution.py:18
  172.6 7.4 %collective-permute-start.3 = (f32[1,8,512]{2,1,0:T(8,128)S(1)}, f32[1,8,512]{2,1,0:T(8,128)S(1)}, u32[]{:S(2)}, u32[]{:S(2)}) collective-permute-start(f32[1,8,512]{2,1,0:T(8,128)S(1)} %slice.66), channel_id=1, source_target_pairs={{30,0},{0,2},{2,4},{4,6},{6,8},{8,10},{10,12},{12,14},{14,16},{16,... | collective-permute-start | bytes 49160 | tf_op jit(solution)/shard_map/ppermute | solution.py:18
  174.7 5.3 %copy-start.9 = (f32[140,8,512]{2,1,0:T(8,128)S(1)}, f32[140,8,512]{2,1,0:T(8,128)}, u32[]{:S(2)}) copy-start(f32[140,8,512]{2,1,0:T(8,128)} %param.34) | copy-start | bytes 6881284
  175.3 4.7 %copy-start.34 = (f32[140]{0:T(256)S(1)}, f32[140]{0:T(256)}, u32[]{:S(2)}) copy-start(f32[140]{0:T(256)} %copy-done.33) | copy-start | bytes 1684
  306.9 5.4 %copy-start.1 = (f32[512,1024]{1,0:T(8,128)S(1)}, f32[512,1024]{1,0:T(8,128)}, u32[]{:S(2)}) copy-start(f32[512,1024]{1,0:T(8,128)} %copy-done) | copy-start | bytes 6291460
  306.9 5.4 %copy-start.22 = (f32[140,1024]{1,0:T(8,128)S(1)}, f32[140,1024]{1,0:T(8,128)}, u32[]{:S(2)}) copy-start(f32[140,1024]{1,0:T(8,128)} %all_gather.15) | copy-start | bytes 1720324
  312.2 3.7 %collective-permute-start.7 = (f32[1,8,512]{2,1,0:T(8,128)S(1)}, f32[1,8,512]{2,1,0:T(8,128)S(1)}, u32[]{:S(2)}, u32[]{:S(2)}) collective-permute-start(f32[1,8,512]{2,1,0:T(8,128)S(1)} %slice.75), channel_id=1, source_target_pairs={{2,0},{4,2},{6,4},{8,6},{10,8},{12,10},{14,12},{16,14},{18,16},{20... | collective-permute-start | bytes 49160 | tf_op jit(solution)/shard_map/ppermute | solution.py:18
  314.6 3.6 %collective-permute-start.6 = (f32[1,512]{1,0:T(1,128)S(1)}, f32[1,512]{1,0:T(1,128)S(1)}, u32[]{:S(2)}, u32[]{:S(2)}) collective-permute-start(f32[1,512]{1,0:T(1,128)S(1)} %slice.73), channel_id=1, source_target_pairs={{2,0},{4,2},{6,4},{8,6},{10,8},{12,10},{14,12},{16,14},{18,16},{20... | collective-permute-start | bytes 6152 | tf_op jit(solution)/shard_map/ppermute | solution.py:18
  (22 other events, 41.7 us)
where the time goes:
time: 320 us; the launch traced here: 319 us
  blocking collectives  236 us (74%)
  other arithmetic  34 us (11%)
  matrix products  13.8 us (4%)
  starting transfers between devices  13 us (4%)
  local copies, waits for them, and re-layouts  8.49 us (3%)
  between operations  8.08 us (3%)
  waiting for transfers between devices  5.53 us (2%)
    psum x2, blocking collectives, per_device(): invest = lax.psum(invest_part, 'hour')  151 us
    psum x2, blocking collectives, per_device(): squares = lax.psum(square_part, ('hour', 'region'))  74.5 us
    dot_general x4, matrix products, fold_part(): lax.dot_general(segment, matrix, (((1,), (1,)), ((), ())), precision=lax....  13.8 us
    ppermute x8, starting transfers between devices, shifted(): return lax.ppermute(block, axis, route)  13 us
  transfers between devices with their start and end apart: 8, of which 2 were waited for; matrix products, arithmetic and copies ran while one was open for 11% of the time, Pallas kernels for 0%

commit v1 on v0

--- a/solution.py
+++ b/solution.py
@@ -91,7 +91,10 @@
         )
         invest_part = jnp.sum(available * limit_dual + ramp_rate[None] * ramp_dual, axis=0)
         invest = lax.psum(invest_part, "hour")
-        squares = lax.psum(square_part, ("hour", "region"))
+        follow_slices = lambda message, link_axis, lane_axis: jax.lax.psum(
+            jax.lax.psum(message, link_axis), lane_axis
+        )
+        squares = follow_slices(square_part, link_axis="region", lane_axis="hour")
         cap_new = jnp.maximum(
             0.0, capacity - capacity_step * (inv_cost - invest / float(total_hours))
         )

time: 320 us -> 248 us (0.78)
  blocking collectives: 236 us -> 161 us
    psum x2, blocking collectives: 74.5 us -> 5.94 us  [per_device(): jax.lax.psum(message, link_axis)]
    psum x2, blocking collectives: 151 us -> 144 us  [per_device(): invest = lax.psum(invest_part, 'hour')]
where the time goes in v1:
time: 248 us; the launch traced here: 247 us
  blocking collectives  161 us (65%)
  other arithmetic  35.8 us (14%)
  starting transfers between devices  14.4 us (6%)
  matrix products  13.9 us (6%)
  between operations  8.3 us (3%)
  waiting for transfers between devices  7.44 us (3%)
  local copies, waits for them, and re-layouts  6.15 us (2%)
    psum x2, blocking collectives, per_device(): invest = lax.psum(invest_part, 'hour')  144 us
    ppermute x8, starting transfers between devices, shifted(): return lax.ppermute(block, axis, route)  14.4 us
    dot_general x4, matrix products, fold_part(): lax.dot_general(segment, matrix, (((1,), (1,)), ((), ())), precision=lax....  13.9 us
    ppermute x8, waiting for transfers between devices, shifted(): return lax.ppermute(block, axis, route)  7.44 us
    all_gather x2, blocking collectives, per_device(): lax.all_gather(ang_bar, 'region', axis=1, tiled=True)  6.1 us
    psum x2, blocking collectives, per_device(): jax.lax.psum(message, link_axis)  5.94 us
    reduce_sum x1, other arithmetic, per_device(): jnp.sum(gen_bar, axis=1) + pow_bar  5.8 us
    reduce_sum x2, other arithmetic, per_device(): jnp.sum((gen_new - generation) ** 2) + jnp.sum((ang_new - angles) ** 2)  5.61 us
  transfers between devices with their start and end apart: 8, of which 2 were waited for; matrix products, arithmetic and copies ran while one was open for 11% of the time, Pallas kernels for 0%

profile of v1, /device:TPU:0, one launch (start us, length us, event | category | flops | bytes accessed | tf_op | source)
XLA Modules:
  0.0 247.3 jit_solution(16707573921216332136)
XLA Ops:
  1.4 2.9 %collective-permute-start.1 = (f32[1,512]{1,0:T(1,128)S(1)}, f32[1,512]{1,0:T(1,128)S(1)}, u32[]{:S(2)}, u32[]{:S(2)}) collective-permute-start(f32[1,512]{1,0:T(1,128)S(1)} %slice.50), channel_id=1, source_target_pairs={{30,0},{0,2},{2,4},{4,6},{6,8},{8,10},{10,12},{12,14},{14,16},{16,... | collective-permute-start | bytes 6152 | tf_op jit(solution)/shard_map/ppermute | solution.py:18
  7.2 2.4 all_gather.12
  12.2 3.7 %multiply_subtract_fusion.7 = (f32[140,512]{1,0:T(8,128)S(1)}, f32[]{:T(128)}, f32[140,512]{1,0:T(8,128)}) fusion(f32[140,512]{1,0:T(8,128)S(1)} %copy-done.24, f32[512,1024]{1,0:T(8,128)S(1)} %bitcast_multiply_fusion, f32[140,1024]{1,0:T(8,128)S(1)} %all_gather.12), kind=kOutput, calls=%fused_computation.61 | convolution fusion | flops 881305600 | bytes 3530756 | tf_op jit(solution)/shard_map/dot_general | solution.py:63
  15.9 2.2 all_gather.13
  18.1 3.0 %fusion.39 = f32[140,512]{1,0:T(8,128)} fusion(f32[140,1024]{1,0:T(8,128)S(1)} %all_gather.13, f32[512,1024]{1,0:T(8,128)S(1)} %bitcast_multiply_fusion), kind=kOutput, calls=%fused_computation.76 | convolution fusion | flops 880803840 | bytes 2957312 | tf_op jit(solution)/shard_map/dot_general | solution.py:63
  21.9 3.2 %multiply_subtract_fusion.6 = (f32[140,512]{1,0:T(8,128)S(1)}, f32[140,512]{1,0:T(8,128)S(1)}, f32[]{:T(128)}, f32[140,512]{1,0:T(8,128)}) fusion(f32[140,512]{1,0:T(8,128)} %param.29, f32[140,512]{1,0:T(8,128)} %param.33, f32[139,512]{1,0:T(8,128)} %bitcast.22, f32[1,512]{1,0:T(1,128)S(1)} %collective-permute-done.1, f32[140,512]{1,0:T(8,128)} %param.30, ...), kind=kLoop, calls=%fused_computation.59 | loop fusion | flops 931839 | bytes 2293764 | tf_op jit(solution)/shard_map/sub | solution.py:106
  25.2 1.9 multiply_reduce_fusion.5
  27.9 5.8 %fusion.36 = (f32[140,512]{1,0:T(8,128)}, f32[140,8,512]{2,1,0:T(8,128)}, f32[140,8,512]{2,1,0:T(8,128)S(1)}, f32[8,512]{1,0:T(8,128)S(1)}) fusion(f32[140,8,512]{2,1,0:T(8,128)S(1)} %copy-done.8, f32[140,8,512]{2,1,0:T(8,128)S(1)} %copy-done.5, f32[139,8,512]{2,1,0:T(8,128)S(1)} %slice-done, f32[1,8,512]{2,1,0:T(8,128)S(1)} %collective-permute-done, ...), kind=kLoop, calls=%fused_computation.74 | loop fusion | flops 10246144 | bytes 15548976 | tf_op jit(solution)/shard_map/reduce_sum | solution.py:112
  37.7 4.2 %collective-permute-start.4 = (f32[1,512]{1,0:T(1,128)S(1)}, f32[1,512]{1,0:T(1,128)S(1)}, u32[]{:S(2)}, u32[]{:S(2)}) collective-permute-start(f32[1,512]{1,0:T(1,128)S(1)} %slice.69), channel_id=1, source_target_pairs={{2,0},{4,2},{6,4},{8,6},{10,8},{12,10},{14,12},{16,14},{18,16},{20... | collective-permute-start | bytes 6152 | tf_op jit(solution)/shard_map/ppermute | solution.py:18
  41.9 3.0 %psum.42 = f32[]{:T(128)} all-reduce(f32[]{:T(128)S(6)} %add.153), channel_id=1, replica_groups=mesh['hour'=16,'region'=2] {'region'}, use_global_device_ids=true, to_apply=%region_4.0 | all-reduce | flops 1 | bytes 8 | tf_op jit(solution)/shard_map/psum | solution.py:95
  44.8 72.0 %all-reduce.1 = (f32[8,512]{1,0:T(8,128)S(1)}, f32[]{:T(128)}) all-reduce(f32[8,512]{1,0:T(8,128)S(1)} %get-tuple-element.36, f32[]{:T(128)} %psum.42), channel_id=1, replica_groups=mesh['hour'=16,'region'=2] {'hour'}, use_global_device_ids=true, to_apply=%region_8.0 | all-reduce | flops 4097 | bytes 32776 | tf_op jit(solution)/shard_map/psum | solution.py:93
  118.3 3.2 %multiply_reduce_fusion.3 = (f32[]{:T(128)}, f32[140,512]{1,0:T(8,128)}, f32[140,512]{1,0:T(8,128)S(1)}, f32[140,512]{1,0:T(8,128)S(1)}) fusion(f32[140,512]{1,0:T(8,128)} %get-tuple-element.46, f32[140,512]{1,0:T(8,128)} %param.33, f32[140,512]{1,0:T(8,128)} %param.30, f32[140,512]{1,0:T(8,128)} %copy-done.17, f32[1,512]{1,0:T(1,128)S(1)} %collective-permute-done.4, ...), kind=kLoop, calls=%fused_computation.56 | loop fusion | flops 1361919 | bytes 3441208 | tf_op jit(solution)/shard_map/reduce_sum | solution.py:89
  121.5 5.6 %collective-permute-start.2 = (f32[1,8,512]{2,1,0:T(8,128)S(1)}, f32[1,8,512]{2,1,0:T(8,128)S(1)}, u32[]{:S(2)}, u32[]{:S(2)}) collective-permute-start(f32[1,8,512]{2,1,0:T(8,128)S(1)} %slice.65), channel_id=1, source_target_pairs={{2,0},{4,2},{6,4},{8,6},{10,8},{12,10},{14,12},{16,14},{18,16},{20... | collective-permute-start | bytes 49160 | tf_op jit(solution)/shard_map/ppermute | solution.py:18
  127.2 2.4 all_gather.14
  129.6 4.8 %multiply_subtract_fusion.3 = (f32[140,512]{1,0:T(8,128)}, f32[]{:T(128)}, f32[140,512]{1,0:T(8,128)}) fusion(f32[140,512]{1,0:T(8,128)} %get-tuple-element.47, f32[140,1024]{1,0:T(8,128)S(1)} %all_gather.14, f32[512,1024]{1,0:T(8,128)S(1)} %bitcast_multiply_fusion), kind=kOutput, calls=%fused_computation.53 | convolution fusion | flops 881305600 | bytes 3530756 | tf_op jit(solution)/shard_map/dot_general | solution.py:63
  138.1 6.4 %collective-permute-done.3 = f32[1,8,512]{2,1,0:T(8,128)S(1)} collective-permute-done((f32[1,8,512]{2,1,0:T(8,128)S(1)}, f32[1,8,512]{2,1,0:T(8,128)S(1)}, u32[]{:S(2)}, u32[]{:S(2)}) %collective-permute-start.3) | collective-permute-done | bytes 16416 | tf_op jit(solution)/shard_map/ppermute | solution.py:18
  144.5 4.3 %multiply_reduce_fusion = (f32[]{:T(128)}, f32[140,8,512]{2,1,0:T(8,128)}, f32[140,8,512]{2,1,0:T(8,128)}) fusion(f32[140,8,512]{2,1,0:T(8,128)S(1)} %copy-done.3, f32[140,8,512]{2,1,0:T(8,128)S(1)} %fusion.7, f32[139,8,512]{2,1,0:T(8,128)S(1)} %slice.67, f32[1,8,512]{2,1,0:T(8,128)S(1)} %collective-permute-done.3, f32[140,512]{1,0:T(8,128)S(1)} %get-tuple-element.23, ...), kind=kLoop, calls=%fused_computation.22 | loop fusion | flops 10895359 | bytes 17539640 | tf_op jit(solution)/shard_map/reduce_sum | solution.py:87
  151.4 3.9 %all_gather.15 = f32[140,1024]{1,0:T(8,128)} all-gather(f32[140,512]{1,0:T(8,128)} %get-tuple-element.41), channel_id=1, replica_groups=mesh['hour'=16,'region'=2] {'region'}, dimensions={1}, use_global_device_ids=true | all-gather | bytes 860160 | tf_op jit(solution)/shard_map/all_gather | solution.py:114
  155.3 3.0 %psum.46 = f32[]{:T(128)} all-reduce(f32[]{:T(128)S(6)} %add.173), channel_id=1, replica_groups=mesh['hour'=16,'region'=2] {'region'}, use_global_device_ids=true, to_apply=%region_15.0 | all-reduce | flops 1 | bytes 8 | tf_op jit(solution)/shard_map/psum | solution.py:95
  158.3 2.2 add_reduce_fusion
  160.5 72.4 %all-reduce = (f32[8,512]{1,0:T(8,128)}, f32[]{:T(128)}) all-reduce(f32[8,512]{1,0:T(8,128)S(1)} %add_reduce_fusion, f32[]{:T(128)} %psum.46), channel_id=1, replica_groups=mesh['hour'=16,'region'=2] {'hour'}, use_global_device_ids=true, to_apply=%region_10.0 | all-reduce | flops 4097 | bytes 32776 | tf_op jit(solution)/shard_map/psum | solution.py:93
  234.9 5.3 %add_maximum_fusion = (f32[140,8,512]{2,1,0:T(8,128)}, f32[140,8,512]{2,1,0:T(8,128)S(1)}) fusion(f32[140,8,512]{2,1,0:T(8,128)} %get-tuple-element.26, bf16[140,8,512]{2,1,0:T(8,128)(2,1)S(1)} %copy-done.7, f32[8,512]{1,0:T(8,128)S(1)} %get-tuple-element.14, f32[]{:T(128)S(6)} %div.23, f32[140]{0:T(256)S(1)} %copy-done.31, ...), kind=kLoop, calls=%fused_computation.20 | loop fusion | flops 5734400 | bytes 12649012 | tf_op jit(solution)/shard_map/max | solution.py:118
  240.3 2.3 fusion.40
  244.0 2.3 fusion.15
  (106 shorter events, 16.5 us)
Async XLA Ops:
  1.4 20.6 %collective-permute-start.1 = (f32[1,512]{1,0:T(1,128)S(1)}, f32[1,512]{1,0:T(1,128)S(1)}, u32[]{:S(2)}, u32[]{:S(2)}) collective-permute-start(f32[1,512]{1,0:T(1,128)S(1)} %slice.50), channel_id=1, source_target_pairs={{30,0},{0,2},{2,4},{4,6},{6,8},{8,10},{10,12},{12,14},{14,16},{16,... | collective-permute-start | bytes 6152 | tf_op jit(solution)/shard_map/ppermute | solution.py:18
  5.0 22.8 %collective-permute-start = (f32[1,8,512]{2,1,0:T(8,128)S(1)}, f32[1,8,512]{2,1,0:T(8,128)S(1)}, u32[]{:S(2)}, u32[]{:S(2)}) collective-permute-start(f32[1,8,512]{2,1,0:T(8,128)S(1)} %slice.48), channel_id=1, source_target_pairs={{30,0},{0,2},{2,4},{4,6},{6,8},{8,10},{10,12},{12,14},{14,16},{16,... | collective-permute-start | bytes 49160 | tf_op jit(solution)/shard_map/ppermute | solution.py:18
  12.2 117.4 %copy-start = (f32[512,1024]{1,0:T(8,128)}, f32[512,1024]{1,0:T(8,128)S(1)}, u32[]{:S(2)}) copy-start(f32[512,1024]{1,0:T(8,128)S(1)} %bitcast_multiply_fusion) | copy-start | bytes 6291460
  21.2 97.1 %copy-start.29 = (f32[140]{0:T(256)}, f32[140]{0:T(256)S(1)}, u32[]{:S(2)}) copy-start(f32[140]{0:T(256)S(1)} %compare_convert_fusion) | copy-start | bytes 1684
  21.2 6.7 %copy-start.5 = (f32[140,8,512]{2,1,0:T(8,128)S(1)}, f32[140,8,512]{2,1,0:T(8,128)}, u32[]{:S(2)}) copy-start(f32[140,8,512]{2,1,0:T(8,128)} %param.35) | copy-start | bytes 6881284
  21.2 6.7 %copy-start.8 = (f32[140,8,512]{2,1,0:T(8,128)S(1)}, f32[140,8,512]{2,1,0:T(8,128)}, u32[]{:S(2)}) copy-start(f32[140,8,512]{2,1,0:T(8,128)} %param.27) | copy-start | bytes 6881284
  21.9 6.0 %copy-start.7 = (bf16[140,8,512]{2,1,0:T(8,128)(2,1)S(1)}, bf16[140,8,512]{2,1,0:T(8,128)(2,1)}, u32[]{:S(2)}) copy-start(bf16[140,8,512]{2,1,0:T(8,128)(2,1)} %param.19) | copy-start | bytes 3440644
  21.9 6.0 %copy-start.25 = (f32[8,512]{1,0:T(8,128)S(1)}, f32[8,512]{1,0:T(8,128)}, u32[]{:S(2)}) copy-start(f32[8,512]{1,0:T(8,128)} %param.23) | copy-start | bytes 49156
  21.9 6.0 %copy-start.28 = (f32[8,512]{1,0:T(8,128)S(1)}, f32[8,512]{1,0:T(8,128)}, u32[]{:S(2)}) copy-start(f32[8,512]{1,0:T(8,128)} %param.21) | copy-start | bytes 49156
  37.7 80.5 %collective-permute-start.4 = (f32[1,512]{1,0:T(1,128)S(1)}, f32[1,512]{1,0:T(1,128)S(1)}, u32[]{:S(2)}, u32[]{:S(2)}) collective-permute-start(f32[1,512]{1,0:T(1,128)S(1)} %slice.69), channel_id=1, source_target_pairs={{2,0},{4,2},{6,4},{8,6},{10,8},{12,10},{14,12},{16,14},{18,16},{20... | collective-permute-start | bytes 6152 | tf_op jit(solution)/shard_map/ppermute | solution.py:18
  121.5 13.2 %copy-start.10 = (f32[140,512]{1,0:T(8,128)}, f32[140,512]{1,0:T(8,128)S(1)}, u32[]{:S(2)}) copy-start(f32[140,512]{1,0:T(8,128)S(1)} %get-tuple-element.22) | copy-start | bytes 860164
  121.5 23.0 %copy-start.14 = (f32[140,512]{1,0:T(8,128)}, f32[140,512]{1,0:T(8,128)S(1)}, u32[]{:S(2)}) copy-start(f32[140,512]{1,0:T(8,128)S(1)} %get-tuple-element.23) | copy-start | bytes 860164
  121.5 12.9 %copy-start.26 = (f32[8,512]{1,0:T(8,128)S(1)}, f32[8,512]{1,0:T(8,128)}, u32[]{:S(2)}) copy-start(f32[8,512]{1,0:T(8,128)} %param.31) | copy-start | bytes 49156
  121.5 12.9 %copy-start.27 = (f32[8,512]{1,0:T(8,128)S(1)}, f32[8,512]{1,0:T(8,128)}, u32[]{:S(2)}) copy-start(f32[8,512]{1,0:T(8,128)} %param.22) | copy-start | bytes 49156
  121.5 12.9 %copy-start.4 = (f32[140,8,512]{2,1,0:T(8,128)S(1)}, f32[140,8,512]{2,1,0:T(8,128)}, u32[]{:S(2)}) copy-start(f32[140,8,512]{2,1,0:T(8,128)} %get-tuple-element.30) | copy-start | bytes 6881284
  121.5 13.1 %collective-permute-start.5 = (f32[1,512]{1,0:T(1,128)S(1)}, f32[1,512]{1,0:T(1,128)S(1)}, u32[]{:S(2)}, u32[]{:S(2)}) collective-permute-start(f32[1,512]{1,0:T(1,128)S(1)} %slice.70), channel_id=1, source_target_pairs={{30,0},{0,2},{2,4},{4,6},{6,8},{8,10},{10,12},{12,14},{14,16},{16,... | collective-permute-start | bytes 6152 | tf_op jit(solution)/shard_map/ppermute | solution.py:18
  121.5 14.6 %collective-permute-start.2 = (f32[1,8,512]{2,1,0:T(8,128)S(1)}, f32[1,8,512]{2,1,0:T(8,128)S(1)}, u32[]{:S(2)}, u32[]{:S(2)}) collective-permute-start(f32[1,8,512]{2,1,0:T(8,128)S(1)} %slice.65), channel_id=1, source_target_pairs={{2,0},{4,2},{6,4},{8,6},{10,8},{12,10},{14,12},{16,14},{18,16},{20... | collective-permute-start | bytes 49160 | tf_op jit(solution)/shard_map/ppermute | solution.py:18
  137.0 7.4 %collective-permute-start.3 = (f32[1,8,512]{2,1,0:T(8,128)S(1)}, f32[1,8,512]{2,1,0:T(8,128)S(1)}, u32[]{:S(2)}, u32[]{:S(2)}) collective-permute-start(f32[1,8,512]{2,1,0:T(8,128)S(1)} %slice.66), channel_id=1, source_target_pairs={{30,0},{0,2},{2,4},{4,6},{6,8},{8,10},{10,12},{12,14},{14,16},{16,... | collective-permute-start | bytes 49160 | tf_op jit(solution)/shard_map/ppermute | solution.py:18
  137.1 7.3 %copy-start.9 = (f32[140,8,512]{2,1,0:T(8,128)S(1)}, f32[140,8,512]{2,1,0:T(8,128)}, u32[]{:S(2)}) copy-start(f32[140,8,512]{2,1,0:T(8,128)} %param.34) | copy-start | bytes 6881284
  137.9 6.6 %copy-start.3 = (f32[140,8,512]{2,1,0:T(8,128)S(1)}, f32[140,8,512]{2,1,0:T(8,128)}, u32[]{:S(2)}) copy-start(f32[140,8,512]{2,1,0:T(8,128)} %copy-done.2) | copy-start | bytes 6881284
  137.9 6.6 %copy-start.30 = (f32[140]{0:T(256)S(1)}, f32[140]{0:T(256)}, u32[]{:S(2)}) copy-start(f32[140]{0:T(256)} %copy-done.29) | copy-start | bytes 1684
  158.3 76.6 %copy-start.31 = (f32[140]{0:T(256)S(1)}, f32[140]{0:T(256)}, u32[]{:S(2)}) copy-start(f32[140]{0:T(256)} %copy-done.29) | copy-start | bytes 1684
  240.2 3.7 %collective-permute-start.7 = (f32[1,8,512]{2,1,0:T(8,128)S(1)}, f32[1,8,512]{2,1,0:T(8,128)S(1)}, u32[]{:S(2)}, u32[]{:S(2)}) collective-permute-start(f32[1,8,512]{2,1,0:T(8,128)S(1)} %slice.75), channel_id=1, source_target_pairs={{2,0},{4,2},{6,4},{8,6},{10,8},{12,10},{14,12},{16,14},{18,16},{20... | collective-permute-start | bytes 49160 | tf_op jit(solution)/shard_map/ppermute | solution.py:18
  242.7 3.6 %collective-permute-start.6 = (f32[1,512]{1,0:T(1,128)S(1)}, f32[1,512]{1,0:T(1,128)S(1)}, u32[]{:S(2)}, u32[]{:S(2)}) collective-permute-start(f32[1,512]{1,0:T(1,128)S(1)} %slice.73), channel_id=1, source_target_pairs={{2,0},{4,2},{6,4},{8,6},{10,8},{12,10},{14,12},{16,14},{18,16},{20... | collective-permute-start | bytes 6152 | tf_op jit(solution)/shard_map/ppermute | solution.py:18
  (18 other events, 44.3 us)
